TPU v7x, 768 devices: a whole 4x8x12 slice. The times are simulated.
768 devices in a mesh: dp: 24 (over z, core), vocab: 32 (over y, x).
Axes of the slice: x: 4, y: 8, z: 12, core: 2. Of those that a mesh axis runs over, the one named last changes fastest.
Arguments:
- tokens_in: bfloat16 [3072, 8192], P('dp'), may hold values from -80 to 80
- gain: float32 [8192], replicated, may hold values from 0.5 to 1.5
- head_weight: bfloat16 [8192, 16896], P(None, 'vocab'), may hold values from -0.5 to 0.5
- teacher_ids: int32 [3072, 16], P('dp'), may hold values from 0 to 16895
- teacher_weight: float32 [3072, 16], P('dp'), may hold values from 0.05 to 1
- labels: int32 [3072], P('dp'), may hold values from 0 to 16895
Outputs:
- token_loss: float32 [3072], P('dp')
- grad_input: bfloat16 [3072, 8192], P('dp', 'vocab')
- head_grad: float32 [528, 32, 8192], P('dp', 'vocab')
All inputs are finite; a program needn't handle non-finite values.
Results may differ from a plain program's by a relative error of at most 0.015.
Values may be sent and summed in bfloat16 or wider, within the bound.
No kernel may reach another device: no remote copies, remote signals or barrier semaphores. Data moves between devices by JAX's collectives and lax.ppermute only.
A program may use at most 64 MiB of HBM per device.

v0:
```python
import jax
import jax.numpy as jnp
from jax import lax
from jax.experimental import pallas as pl
from jax.experimental.pallas import tpu as pltpu
from jax.sharding import Mesh, PartitionSpec as P


LABEL_SHARE = 0.5
EPS = 1e-05
NZ, NC, NY, NX = 12, 2, 8, 4


def front_kernel(
    start_ref, x_hbm, gain_ref, w_hbm, ids_ref, weight_ref, label_ref,
    normed_hbm, scale_ref, logits_ref, target_ref, stats_ref,
    x_buf, w_ref, normed_buf, x_sem, w_sem, out_sem,
):
    tokens, features = x_buf.shape
    cols = w_ref.shape[0]
    parts = w_sem.shape[0]
    rows = cols // parts
    lines = 16
    copy_x = pltpu.make_async_copy(x_hbm, x_buf, x_sem)
    copy_x.start()

    def copy_w(p):
        part = pl.ds(p * rows, rows)
        return pltpu.make_async_copy(w_hbm.at[part], w_ref.at[part], w_sem.at[p])

    @pl.loop(0, parts)
    def _(p):
        copy_w(p).start()

    probs = weight_ref[...] / jnp.sum(weight_ref[...], axis=0, keepdims=True)

    @pl.loop(0, cols // lines)
    def _(r):
        part = pl.ds(pl.multiple_of(r * lines, lines), lines)
        columns = start_ref[0] + r * lines + lax.broadcasted_iota(jnp.int32, (lines, tokens), 0)
        teacher_part = jnp.zeros((lines, tokens), jnp.float32)
        for k in range(ids_ref.shape[0]):
            teacher_part += jnp.where(ids_ref[k : k + 1, :] == columns, probs[k : k + 1, :], 0.0)
        label_part = jnp.where(label_ref[...] == columns, LABEL_SHARE, 0.0)
        target_ref[part, :] = (1.0 - LABEL_SHARE) * teacher_part + label_part

    copy_x.wait()

    @pl.loop(0, tokens // lines)
    def _(r):
        part = pl.ds(pl.multiple_of(r * lines, lines), lines)
        totals = [jnp.zeros((lines, 128), jnp.float32) for _ in range(4)]
        for f in range(0, features, 128):
            chunk = x_buf[part, f : f + 128].astype(jnp.float32)
            totals[f // 128 % 4] += chunk * chunk
        total = (totals[0] + totals[1]) + (totals[2] + totals[3])
        scale = jnp.sqrt(jnp.sum(total, axis=1, keepdims=True) / features + EPS)
        scale_ref[part, :] = scale
        inverse = jnp.broadcast_to(1.0 / scale, (lines, 128))
        for f in range(0, features, 128):
            chunk = x_buf[part, f : f + 128].astype(jnp.float32)
            chunk = chunk * inverse * gain_ref[:, f : f + 128]
            normed_buf[part, f : f + 128] = chunk.astype(jnp.bfloat16)

    copy_out = pltpu.make_async_copy(normed_buf, normed_hbm, out_sem)
    copy_out.start()
    for p in range(parts):
        copy_w(p).wait()
        part = pl.ds(p * rows, rows)
        logits_ref[part, :] = lax.dot_general(
            w_ref[part, :],
            normed_buf[...],
            (((1,), (1,)), ((), ())),
            preferred_element_type=jnp.float32,
        )
    logits = logits_ref[...]
    top = jnp.max(logits, axis=0, keepdims=True)
    exps = jnp.exp(logits - top)
    local_stats = (
        top,
        jnp.sum(exps, axis=0, keepdims=True),
        jnp.sum(target_ref[...] * logits, axis=0, keepdims=True),
        jnp.sum(exps * logits, axis=0, keepdims=True),
    )
    for q, row in enumerate(local_stats):
        stats_ref[:, q, :] = jnp.broadcast_to(row, (stats_ref.shape[0], tokens))
    copy_out.wait()


def front(tokens_in, gain, weight_t, ids_t, teacher_t, labels, start, n_vocab):
    tokens, features = tokens_in.shape
    cols = weight_t.shape[0]
    vmem = pl.BlockSpec(memory_space=pltpu.VMEM)
    hbm = pl.BlockSpec(memory_space=pltpu.HBM)
    return pl.pallas_call(
        front_kernel,
        name="front",
        out_shape=(
            jax.ShapeDtypeStruct((tokens, features), jnp.bfloat16),
            jax.ShapeDtypeStruct((tokens, 1), jnp.float32),
            jax.ShapeDtypeStruct((cols, tokens), jnp.float32),
            jax.ShapeDtypeStruct((cols, tokens), jnp.float32),
            jax.ShapeDtypeStruct((n_vocab, 4, tokens), jnp.float32),
        ),
        in_specs=[pl.BlockSpec(memory_space=pltpu.SMEM), hbm, vmem, hbm, vmem, vmem, vmem],
        out_specs=(hbm, vmem, vmem, vmem, vmem),
        scratch_shapes=[
            pltpu.VMEM((tokens, features), jnp.bfloat16),
            pltpu.VMEM((cols, features), jnp.bfloat16),
            pltpu.VMEM((tokens, features), jnp.bfloat16),
            pltpu.SemaphoreType.DMA,
            pltpu.SemaphoreType.DMA((3,)),
            pltpu.SemaphoreType.DMA,
        ],
        cost_estimate=pl.CostEstimate(
            flops=2 * tokens * features * cols,
            bytes_accessed=2 * features * (2 * tokens + cols),
            transcendentals=cols * tokens,
        ),
    )(start, tokens_in, gain, weight_t, ids_t, teacher_t, labels)


def local(tokens_in, gain, head_weight, teacher_ids, teacher_weight, labels):
    tokens, features = tokens_in.shape
    col_width = head_weight.shape[1]
    n_vocab = NY * NX
    block = lax.axis_index("y") * NX + lax.axis_index("x")
    core = lax.axis_index("c")
    swap = [(0, 1), (1, 0)]
    weight_t = head_weight.T
    start = (block * col_width).astype(jnp.int32).reshape(1)
    normed, row_scale, logits, target, stats = front(
        tokens_in, gain[None], weight_t, teacher_ids.T, teacher_weight.T, labels[None], start, n_vocab
    )
    both = jnp.concatenate([normed, lax.ppermute(normed, "c", swap)], axis=0)
    teacher_probs = teacher_weight / jnp.sum(teacher_weight, axis=1, keepdims=True)
    stats = lax.all_to_all(stats, ("y", "x"), 0, 0)
    row_top = jnp.max(stats[:, 0], axis=0)
    weight = jnp.exp(stats[:, 0] - row_top[None])
    total_exp = jnp.sum(weight * stats[:, 1], axis=0)
    total_dot = jnp.sum(stats[:, 2], axis=0)
    mean_logit = jnp.sum(weight * stats[:, 3], axis=0) / total_exp
    lse = row_top + jnp.log(total_exp)
    token_loss = (
        (1.0 - LABEL_SHARE) * jnp.sum(teacher_probs * jnp.log(teacher_probs), axis=1)
        - total_dot
        + lse
    )
    dlogits = (jnp.exp(logits - lse[None]) - target).astype(jnp.bfloat16)

    rows = col_width // (NZ * NC)
    by_owner = jnp.pad(dlogits.reshape(NZ, NC, rows, tokens), ((0, 0), (0, 0), (0, 1), (0, 0)))
    mine = lax.dynamic_index_in_dim(by_owner, core, 1, False).reshape(-1, tokens)
    theirs = lax.dynamic_index_in_dim(by_owner, 1 - core, 1, False).reshape(-1, tokens)
    other_mine = lax.ppermute(theirs, "c", swap)

    width = features // n_vocab
    partial_value = lax.dot_general(
        dlogits, weight_t, (((0,), (0,)), ((), ())), preferred_element_type=jnp.float32
    ).astype(jnp.bfloat16)
    pieces = partial_value.reshape(tokens, n_vocab, width).transpose(1, 0, 2)
    pieces = lax.all_to_all(pieces, ("y", "x"), 0, 0)

    factor = jnp.concatenate([mine, other_mine], axis=1)
    head_term = jnp.dot(factor, both, preferred_element_type=jnp.float32)
    summed = lax.psum_scatter(head_term.astype(jnp.bfloat16), "z", scatter_dimension=0, tiled=True)
    summed = lax.optimization_barrier(summed)
    head_grad = summed[:rows].astype(jnp.float32)[:, None, :]

    dhidden = jnp.sum(pieces.astype(jnp.float32), axis=0)
    local_tokens = lax.dynamic_slice_in_dim(tokens_in, block * width, width, 1).astype(jnp.float32)
    local_gain = lax.dynamic_slice_in_dim(gain, block * width, width, 0)
    inner_sum = row_scale * (mean_logit - total_dot)[:, None]
    cubed = row_scale * row_scale * row_scale
    grad_input = (
        dhidden * local_gain[None, :] / row_scale - local_tokens * inner_sum / (features * cubed)
    ).astype(jnp.bfloat16)
    return (token_loss, grad_input, head_grad)


def solution(mesh):
    fine = Mesh(mesh.devices.reshape(NZ, NC, NY, NX), ("z", "c", "y", "x"))
    dp, vocab = ("z", "c"), ("y", "x")
    in_specs = (P(dp, None), P(), P(None, vocab), P(dp, None), P(dp, None), P(dp))
    out_specs = (P(dp), P(dp, vocab), P(dp, vocab, None))
    return jax.shard_map(local, mesh=fine, in_specs=in_specs, out_specs=out_specs, check_vma=False)
```

profile of v0, /device:TPU:64, one launch (start us, length us, event | category | flops | bytes accessed | tf_op | source)
XLA Modules:
  0.0 132.9 jit_solution(7271795419305365566)
XLA Ops:
  0.6 0.0 copy-start
  0.6 9.0 %front.1 = (bf16[128,8192]{1,0:T(8,128)(2,1)}, f32[128,1]{1,0:T(8,128)}, f32[528,128]{1,0:T(8,128)}, f32[528,128]{1,0:T(8,128)}, f32[32,4,128]{2,1,0:T(4,128)}) custom-call(s32[1]{0:T(128)} %bitcast.start_ref, bf16[128,8192]{1,0:T(8,128)(2,1)} %x_hbm.1, f32[1,8192]{1,0:T(1,128)} %bitcast.40, bf16[528,8192]{1,0:T(8,128)(2,1)} %bitcast.32, ...), custom_call_target="tpu_custom_call" | custom-call | flops 1107296256 | bytes 12845056 | tf_op jit(solution)/shard_map/front/pallas_call | solution.py:95
  9.7 1.9 %collective-permute-start.1 = (bf16[128,8192]{1,0:T(8,128)(2,1)}, bf16[128,8192]{1,0:T(8,128)(2,1)}, u32[]{:S(2)}, u32[]{:S(2)}) collective-permute-start(bf16[128,8192]{1,0:T(8,128)(2,1)} %get-tuple-element.12), channel_id=1, source_target_pairs={{0,32},{32,0},{1,33},{33,1},{2,34},{34,2},{3,35},{35,3},{4,36},{36... | collective-permute-start | bytes 6291464 | tf_op jit(solution)/shard_map/ppermute | solution.py:135
  11.6 10.0 %all-to-all-start = ((f32[32,4,128]{2,1,0:T(4,128)}), f32[32,4,128]{2,1,0:T(4,128)S(1)}, u32[]{:S(2)}, u32[]{:S(2)}) async-start(f32[32,4,128]{2,1,0:T(4,128)} %get-tuple-element.8), calls=%async_computation | async-start | bytes 131072 | tf_op jit(solution)/shard_map/all_to_all | solution.py:137
  21.6 0.0 copy-done
  21.6 9.9 %all-to-all-done = f32[32,4,128]{2,1,0:T(4,128)S(1)} async-done(((f32[32,4,128]{2,1,0:T(4,128)}), f32[32,4,128]{2,1,0:T(4,128)S(1)}, u32[]{:S(2)}, u32[]{:S(2)}) %all-to-all-start) | async-done | bytes 65568 | tf_op jit(solution)/shard_map/all_to_all | solution.py:137
  31.5 0.1 fusion.13
  31.6 0.5 subtract_add_fusion
  32.2 1.1 subtract_convert_fusion
  33.4 1.9 %collective-permute-start = (bf16[276,128]{1,0:T(8,128)(2,1)S(1)}, bf16[276,128]{1,0:T(8,128)(2,1)S(1)}, u32[]{:S(2)}, u32[]{:S(2)}) collective-permute-start(bf16[276,128]{1,0:T(8,128)(2,1)S(1)} %reshape.56), channel_id=1, source_target_pairs={{0,32},{32,0},{1,33},{33,1},{2,34},{34,2},{3,35},{35,3},{4,36},{36... | collective-permute-start | bytes 211976 | tf_op jit(solution)/shard_map/ppermute | solution.py:155
  35.3 5.3 %convolution_convert_fusion.1 = bf16[128,8192]{1,0:T(8,128)(2,1)S(1)} fusion(bf16[528,128]{1,0:T(8,128)(2,1)S(1)} %subtract_convert_fusion, bf16[8192,528]{0,1:T(8,128)(2,1)} %param.8), kind=kOutput, calls=%fused_computation.1 | convolution fusion | flops 1108344832 | bytes 10883072 | tf_op jit(solution)/shard_map/dot_general | solution.py:158
  40.6 1.7 %copy.26 = bf16[16,32,8,256]{3,2,0,1:T(8,128)(2,1)} copy(bf16[16,32,8,256]{3,2,1,0:T(8,128)(2,1)S(1)} %bitcast.33) | data formatting | bytes 4194304 | tf_op jit(solution)/shard_map/reshape | solution.py:161
  42.3 4.0 %all-to-all-start.1 = ((bf16[32,128,256]{2,1,0:T(8,128)(2,1)}), bf16[32,128,256]{2,1,0:T(8,128)(2,1)S(1)}, u32[]{:S(2)}, u32[]{:S(2)}) async-start(bf16[32,128,256]{2,1,0:T(8,128)(2,1)} %bitcast.34), calls=%async_computation.1 | async-start | bytes 4194304 | tf_op jit(solution)/shard_map/all_to_all | solution.py:162
  46.4 0.0 collective-permute-done
  46.4 0.0 collective-permute-done.1
  46.4 5.7 %convolution_convert_fusion = bf16[276,8192]{1,0:T(8,128)(2,1)} fusion(bf16[128,8192]{1,0:T(8,128)(2,1)} %collective-permute-done.1, bf16[128,8192]{1,0:T(8,128)(2,1)} %get-tuple-element.12, bf16[276,128]{1,0:T(8,128)(2,1)S(1)} %collective-permute-done, bf16[276,128]{1,0:T(8,128)(2,1)S(1)} %reshape.55), kind=kOutput, calls=%fused_computation | convolution fusion | flops 1168560128 | bytes 8857600 | tf_op jit(solution)/shard_map/dot_general | solution.py:165
  52.0 66.6 %fusion = bf16[24,8192]{1,0:T(8,128)(2,1)S(1)} fusion(bf16[276,8192]{1,0:T(8,128)(2,1)} %convolution_convert_fusion), kind=kCustom, calls=%all-reduce-scatter | all-reduce-scatter fusion | flops 2359297 | bytes 4919296
  118.7 0.1 slice.26
  118.7 1.9 %collective-permute-start.2 = (bf16[11,8192]{1,0:T(8,128)(2,1)S(1)}, bf16[11,8192]{1,0:T(8,128)(2,1)S(1)}, u32[]{:S(2)}, u32[]{:S(2)}) collective-permute-start(bf16[11,8192]{1,0:T(8,128)(2,1)S(1)} %slice.26), channel_id=1, source_target_pairs={{0,64},{64,128},{128,192},{192,256},{256,320},{320,384},{384,448},... | collective-permute-start | bytes 540680
  120.7 0.8 dynamic_slice.13
  121.4 1.3 dynamic-slice.4
  123.3 0.1 copy.20
  123.5 0.0 copy-done.1
  123.5 0.1 fusion.12
  123.6 4.9 %collective-permute-done.2 = bf16[11,8192]{1,0:T(8,128)(2,1)S(1)} collective-permute-done((bf16[11,8192]{1,0:T(8,128)(2,1)S(1)}, bf16[11,8192]{1,0:T(8,128)(2,1)S(1)}, u32[]{:S(2)}, u32[]{:S(2)}) %collective-permute-start.2) | collective-permute-done | bytes 180256
  128.5 0.8 concatenate.8
  129.3 0.1 constant_dynamic-slice_fusion
  129.4 0.1 fusion.4
  129.4 1.6 %copy.21 = f32[22,1,8192]{2,1,0:T(1,128)} copy(f32[22,1,8192]{2,0,1:T(8,128)S(1)} %fusion.4) | data formatting | bytes 1441792
  131.0 0.0 all-to-all-done.1
  131.0 0.3 convert_reduce_fusion
  131.3 1.6 %subtract_convert_fusion.1 = bf16[128,256]{1,0:T(8,128)(2,1)} fusion(f32[128,256]{1,0:T(8,128)S(1)} %convert_reduce_fusion, f32[128]{0:T(128)S(1)} %get-tuple-element.23, f32[128]{0:T(128)S(1)} %get-tuple-element.24, bf16[128,8192]{1,0:T(8,128)(2,1)} %x_hbm.1, s32[]{:T(128)S(6)} %select_n.11, f32[128]{0:T(128)S(1)} %get-tuple-element.22, ...), kind=kLoop, calls=%fused_computation.13 | loop fusion | flops 229376 | bytes 264708 | tf_op jit(solution)/shard_map/convert_element_type | solution.py:177
  (9 shorter events, 0.2 us)
Async XLA Ops:
  0.6 20.9 %copy-start = (f32[128,16]{0,1:T(8,128)S(1)}, f32[128,16]{0,1:T(8,128)}, u32[]{:S(2)}) copy-start(f32[128,16]{0,1:T(8,128)} %param.10) | copy-start | bytes 24580
  9.7 36.7 %collective-permute-start.1 = (bf16[128,8192]{1,0:T(8,128)(2,1)}, bf16[128,8192]{1,0:T(8,128)(2,1)}, u32[]{:S(2)}, u32[]{:S(2)}) collective-permute-start(bf16[128,8192]{1,0:T(8,128)(2,1)} %get-tuple-element.12), channel_id=1, source_target_pairs={{0,32},{32,0},{1,33},{33,1},{2,34},{34,2},{3,35},{35,3},{4,36},{36... | collective-permute-start | bytes 6291464 | tf_op jit(solution)/shard_map/ppermute | solution.py:135
  11.6 19.9 %all-to-all-start = ((f32[32,4,128]{2,1,0:T(4,128)}), f32[32,4,128]{2,1,0:T(4,128)S(1)}, u32[]{:S(2)}, u32[]{:S(2)}) async-start(f32[32,4,128]{2,1,0:T(4,128)} %get-tuple-element.8), calls=%async_computation | async-start | bytes 131072 | tf_op jit(solution)/shard_map/all_to_all | solution.py:137
  33.4 13.0 %collective-permute-start = (bf16[276,128]{1,0:T(8,128)(2,1)S(1)}, bf16[276,128]{1,0:T(8,128)(2,1)S(1)}, u32[]{:S(2)}, u32[]{:S(2)}) collective-permute-start(bf16[276,128]{1,0:T(8,128)(2,1)S(1)} %reshape.56), channel_id=1, source_target_pairs={{0,32},{32,0},{1,33},{33,1},{2,34},{34,2},{3,35},{35,3},{4,36},{36... | collective-permute-start | bytes 211976 | tf_op jit(solution)/shard_map/ppermute | solution.py:155
  42.3 88.7 %all-to-all-start.1 = ((bf16[32,128,256]{2,1,0:T(8,128)(2,1)}), bf16[32,128,256]{2,1,0:T(8,128)(2,1)S(1)}, u32[]{:S(2)}, u32[]{:S(2)}) async-start(bf16[32,128,256]{2,1,0:T(8,128)(2,1)} %bitcast.34), calls=%async_computation.1 | async-start | bytes 4194304 | tf_op jit(solution)/shard_map/all_to_all | solution.py:162
  52.0 71.4 %copy-start.1 = (f32[128,1]{1,0:T(8,128)S(1)}, f32[128,1]{1,0:T(8,128)}, u32[]{:S(2)}) copy-start(f32[128,1]{1,0:T(8,128)} %get-tuple-element.11) | copy-start | bytes 1540
  118.7 9.7 %collective-permute-start.2 = (bf16[11,8192]{1,0:T(8,128)(2,1)S(1)}, bf16[11,8192]{1,0:T(8,128)(2,1)S(1)}, u32[]{:S(2)}, u32[]{:S(2)}) collective-permute-start(bf16[11,8192]{1,0:T(8,128)(2,1)S(1)} %slice.26), channel_id=1, source_target_pairs={{0,64},{64,128},{128,192},{192,256},{256,320},{320,384},{384,448},... | collective-permute-start | bytes 540680
where the time goes:
time: 134 us; the launch traced here: 133 us
  blocking collectives  66.6 us (50%)
  starting transfers between devices  19.7 us (15%)
  waiting for transfers between devices  14.8 us (11%)
  matrix products  11 us (8%)
  Pallas kernels  9 us (7%)
  local copies, waits for them, and re-layouts  6.51 us (5%)
  other arithmetic  3.86 us (3%)
  between operations  1.47 us (1%)
    unnamed x1, blocking collectives  66.6 us
    all_to_all x1, starting transfers between devices, local(): stats = lax.all_to_all(stats, ('y', 'x'), 0, 0)  9.96 us
    all_to_all x1, waiting for transfers between devices, local(): stats = lax.all_to_all(stats, ('y', 'x'), 0, 0)  9.91 us
    pallas_call x1, Pallas kernels, front(): pl.pallas_call(front_kernel, name='front', out_shape=(jax.ShapeDtypeStruc...  9 us
    dot_general x1, matrix products, local(): head_term = jnp.dot(factor, both, preferred_element_type=jnp.float32)  5.65 us
    dot_general x1, matrix products, local(): lax.dot_general(dlogits, weight_t, (((0,), (0,)), ((), ())), preferred_el...  5.32 us
    unnamed x1, waiting for transfers between devices  4.85 us
    all_to_all x1, starting transfers between devices, local(): pieces = lax.all_to_all(pieces, ('y', 'x'), 0, 0)  4.01 us
  transfers between devices with their start and end apart: 5, of which 2 were waited for; matrix products, arithmetic and copies ran while one was open for 65% of the time, Pallas kernels for 0%

commit v1 on v0

--- a/solution.py
+++ b/solution.py
@@ -149,7 +149,7 @@
     dlogits = (jnp.exp(logits - lse[None]) - target).astype(jnp.bfloat16)
 
     rows = col_width // (NZ * NC)
-    by_owner = jnp.pad(dlogits.reshape(NZ, NC, rows, tokens), ((0, 0), (0, 0), (0, 1), (0, 0)))
+    by_owner = jnp.pad(dlogits.reshape(NZ, NC, rows, tokens), ((0, 0), (0, 0), (0, 2), (0, 0)))
     mine = lax.dynamic_index_in_dim(by_owner, core, 1, False).reshape(-1, tokens)
     theirs = lax.dynamic_index_in_dim(by_owner, 1 - core, 1, False).reshape(-1, tokens)
     other_mine = lax.ppermute(theirs, "c", swap)
@@ -161,10 +161,11 @@
     pieces = partial_value.reshape(tokens, n_vocab, width).transpose(1, 0, 2)
     pieces = lax.all_to_all(pieces, ("y", "x"), 0, 0)
 
-    factor = jnp.concatenate([mine, other_mine], axis=1)
-    head_term = jnp.dot(factor, both, preferred_element_type=jnp.float32)
+    factor = jnp.concatenate([mine.T, other_mine.T], axis=0)
+    head_term = lax.dot_general(
+        factor, both, (((0,), (0,)), ((), ())), preferred_element_type=jnp.float32
+    )
     summed = lax.psum_scatter(head_term.astype(jnp.bfloat16), "z", scatter_dimension=0, tiled=True)
-    summed = lax.optimization_barrier(summed)
     head_grad = summed[:rows].astype(jnp.float32)[:, None, :]
 
     dhidden = jnp.sum(pieces.astype(jnp.float32), axis=0)

time: 134 us -> 131 us (0.978)
  the two profiles are of different devices: /device:TPU:64 before, /device:TPU:4 now
where the time goes in v1:
time: 131 us; the launch traced here: 130 us
  waiting for transfers between devices  64.1 us (49%)
  starting transfers between devices  22.8 us (17%)
  between operations  14.1 us (11%)
  matrix products  11.1 us (8%)
  Pallas kernels  9 us (7%)
  other arithmetic  4.86 us (4%)
  local copies, waits for them, and re-layouts  4.19 us (3%)
    all_to_all x1, waiting for transfers between devices, local(): pieces = lax.all_to_all(pieces, ('y', 'x'), 0, 0)  48.9 us
    all_to_all x1, starting transfers between devices, local(): stats = lax.all_to_all(stats, ('y', 'x'), 0, 0)  13 us
    pallas_call x1, Pallas kernels, front(): pl.pallas_call(front_kernel, name='front', out_shape=(jax.ShapeDtypeStruc...  9 us
    all_to_all x1, waiting for transfers between devices, local(): stats = lax.all_to_all(stats, ('y', 'x'), 0, 0)  8.22 us
    all_to_all x1, starting transfers between devices, local(): pieces = lax.all_to_all(pieces, ('y', 'x'), 0, 0)  5.93 us
    dot_general x1, matrix products, local(): lax.dot_general(factor, both, (((0,), (0,)), ((), ())), preferred_element...  5.79 us
    reduce_scatter x1, waiting for transfers between devices, local(): lax.psum_scatter(head_term.astype(jnp.bfloat16), 'z', scatter_dimension=0...  5.69 us
    dot_general x1, matrix products, local(): lax.dot_general(dlogits, weight_t, (((0,), (0,)), ((), ())), preferred_el...  5.32 us
  transfers between devices with their start and end apart: 5, of which 4 were waited for; matrix products, arithmetic and copies ran while one was open for 9% of the time, Pallas kernels for 0%

profile of v1, /device:TPU:4, one launch (start us, length us, event | category | flops | bytes accessed | tf_op | source)
XLA Modules:
  0.0 130.2 jit_solution(2400707057810315969)
XLA Ops:
  7.2 0.0 copy-start
  7.2 9.0 %front.1 = (bf16[128,8192]{1,0:T(8,128)(2,1)}, f32[128,1]{1,0:T(8,128)}, f32[528,128]{1,0:T(8,128)}, f32[528,128]{1,0:T(8,128)}, f32[32,4,128]{2,1,0:T(4,128)}) custom-call(s32[1]{0:T(128)} %bitcast.start_ref, bf16[128,8192]{1,0:T(8,128)(2,1)} %x_hbm.1, f32[1,8192]{1,0:T(1,128)} %bitcast.44, bf16[528,8192]{1,0:T(8,128)(2,1)} %bitcast.34, ...), custom_call_target="tpu_custom_call" | custom-call | flops 1107296256 | bytes 12845056 | tf_op jit(solution)/shard_map/front/pallas_call | solution.py:95
  16.2 1.9 %collective-permute-start.1 = (bf16[128,8192]{1,0:T(8,128)(2,1)}, bf16[128,8192]{1,0:T(8,128)(2,1)}, u32[]{:S(2)}, u32[]{:S(2)}) collective-permute-start(bf16[128,8192]{1,0:T(8,128)(2,1)} %get-tuple-element.12), channel_id=1, source_target_pairs={{0,32},{32,0},{1,33},{33,1},{2,34},{34,2},{3,35},{35,3},{4,36},{36... | collective-permute-start | bytes 6291464 | tf_op jit(solution)/shard_map/ppermute | solution.py:135
  18.1 13.0 %all-to-all-start = ((f32[32,4,128]{2,1,0:T(4,128)}), f32[32,4,128]{2,1,0:T(4,128)S(1)}, u32[]{:S(2)}, u32[]{:S(2)}) async-start(f32[32,4,128]{2,1,0:T(4,128)} %get-tuple-element.8), calls=%async_computation | async-start | bytes 131072 | tf_op jit(solution)/shard_map/all_to_all | solution.py:137
  31.1 0.0 reduce-scatter.2.cloned.1.call-start
  31.2 0.0 copy-done
  31.2 8.2 %all-to-all-done = f32[32,4,128]{2,1,0:T(4,128)S(1)} async-done(((f32[32,4,128]{2,1,0:T(4,128)}), f32[32,4,128]{2,1,0:T(4,128)S(1)}, u32[]{:S(2)}, u32[]{:S(2)}) %all-to-all-start) | async-done | bytes 65568 | tf_op jit(solution)/shard_map/all_to_all | solution.py:137
  39.5 0.1 fusion.12
  39.6 0.5 subtract_add_fusion
  40.1 1.1 subtract_convert_fusion
  41.3 1.9 %collective-permute-start = (bf16[288,128]{1,0:T(8,128)(2,1)S(1)}, bf16[288,128]{1,0:T(8,128)(2,1)S(1)}, u32[]{:S(2)}, u32[]{:S(2)}) collective-permute-start(bf16[288,128]{1,0:T(8,128)(2,1)S(1)} %bitcast.40), channel_id=1, source_target_pairs={{0,32},{32,0},{1,33},{33,1},{2,34},{34,2},{3,35},{35,3},{4,36},{36... | collective-permute-start | bytes 221192 | tf_op jit(solution)/shard_map/ppermute | solution.py:155
  43.2 1.2 collective-permute-done
  44.4 0.0 collective-permute-done.1
  44.4 5.8 %convolution_convert_fusion = bf16[288,8192]{1,0:T(8,128)(2,1)} fusion(bf16[128,8192]{1,0:T(8,128)(2,1)} %collective-permute-done.1, bf16[128,8192]{1,0:T(8,128)(2,1)} %get-tuple-element.12, bf16[128,288]{0,1:T(8,128)(2,1)S(1)} %bitcast.47, bf16[128,288]{0,1:T(8,128)(2,1)S(1)} %bitcast.39), kind=kOutput, calls=%fused_computation | convolution fusion | flops 1219002368 | bytes 9060352 | tf_op jit(solution)/shard_map/dot_general | solution.py:165
  50.2 0.0 reduce-scatter.2.cloned.1.call-update
  50.3 5.3 %convolution_convert_fusion.1 = bf16[128,8192]{1,0:T(8,128)(2,1)S(1)} fusion(bf16[528,128]{1,0:T(8,128)(2,1)S(1)} %subtract_convert_fusion, bf16[8192,528]{0,1:T(8,128)(2,1)} %param.8), kind=kOutput, calls=%fused_computation.1 | convolution fusion | flops 1108344832 | bytes 10883072 | tf_op jit(solution)/shard_map/dot_general | solution.py:158
  55.6 0.0 copy-start.1
  55.6 1.6 %copy.26 = bf16[16,32,8,256]{3,2,0,1:T(8,128)(2,1)} copy(bf16[16,32,8,256]{3,2,1,0:T(8,128)(2,1)S(1)} %bitcast.35) | data formatting | bytes 4194304 | tf_op jit(solution)/shard_map/reshape | solution.py:161
  57.2 5.9 %all-to-all-start.1 = ((bf16[32,128,256]{2,1,0:T(8,128)(2,1)}), bf16[32,128,256]{2,1,0:T(8,128)(2,1)S(1)}, u32[]{:S(2)}, u32[]{:S(2)}) async-start(bf16[32,128,256]{2,1,0:T(8,128)(2,1)} %bitcast.36), calls=%async_computation.1 | async-start | bytes 4194304 | tf_op jit(solution)/shard_map/all_to_all | solution.py:162
  63.2 0.8 dynamic_slice.13
  63.9 0.1 copy.20
  64.0 0.0 copy-done.1
  64.1 0.1 fusion.11
  64.2 48.9 %all-to-all-done.1 = bf16[32,128,256]{2,1,0:T(8,128)(2,1)S(1)} async-done(((bf16[32,128,256]{2,1,0:T(8,128)(2,1)}), bf16[32,128,256]{2,1,0:T(8,128)(2,1)S(1)}, u32[]{:S(2)}, u32[]{:S(2)}) %all-to-all-start.1) | async-done | bytes 2097184 | tf_op jit(solution)/shard_map/all_to_all | solution.py:162
  113.1 0.3 convert_reduce_fusion
  113.4 1.6 %subtract_convert_fusion.1 = bf16[128,256]{1,0:T(8,128)(2,1)} fusion(f32[128,256]{1,0:T(8,128)S(1)} %convert_reduce_fusion, f32[128]{0:T(128)S(1)} %get-tuple-element.23, f32[128]{0:T(128)S(1)} %get-tuple-element.24, bf16[128,8192]{1,0:T(8,128)(2,1)} %x_hbm.1, s32[]{:T(128)S(6)} %select_n.11, f32[128]{0:T(128)S(1)} %get-tuple-element.22, ...), kind=kLoop, calls=%fused_computation.13 | loop fusion | flops 229376 | bytes 264708 | tf_op jit(solution)/shard_map/convert_element_type | solution.py:178
  115.0 5.7 %reduce-scatter.2.cloned.1.call-done = bf16[24,8192]{1,0:T(8,128)(2,1)} async-done(((bf16[288,8192]{1,0:T(8,128)(2,1)}), bf16[24,8192]{1,0:T(8,128)(2,1)}) %reduce-scatter.2.cloned.1.call-update) | async-done | bytes 393232 | tf_op jit(solution)/shard_map/reduce_scatter | solution.py:168
  120.7 1.0 fusion.3
  121.7 1.6 %copy.21 = f32[22,1,8192]{2,1,0:T(1,128)} copy(f32[22,1,8192]{2,0,1:T(8,128)S(1)} %fusion.3) | data formatting | bytes 1441792
  (6 shorter events, 0.2 us)
Async XLA Ops:
  7.2 24.0 %copy-start = (f32[128,16]{0,1:T(8,128)S(1)}, f32[128,16]{0,1:T(8,128)}, u32[]{:S(2)}) copy-start(f32[128,16]{0,1:T(8,128)} %param.10) | copy-start | bytes 24580
  16.2 28.2 %collective-permute-start.1 = (bf16[128,8192]{1,0:T(8,128)(2,1)}, bf16[128,8192]{1,0:T(8,128)(2,1)}, u32[]{:S(2)}, u32[]{:S(2)}) collective-permute-start(bf16[128,8192]{1,0:T(8,128)(2,1)} %get-tuple-element.12), channel_id=1, source_target_pairs={{0,32},{32,0},{1,33},{33,1},{2,34},{34,2},{3,35},{35,3},{4,36},{36... | collective-permute-start | bytes 6291464 | tf_op jit(solution)/shard_map/ppermute | solution.py:135
  18.1 21.3 %all-to-all-start = ((f32[32,4,128]{2,1,0:T(4,128)}), f32[32,4,128]{2,1,0:T(4,128)S(1)}, u32[]{:S(2)}, u32[]{:S(2)}) async-start(f32[32,4,128]{2,1,0:T(4,128)} %get-tuple-element.8), calls=%async_computation | async-start | bytes 131072 | tf_op jit(solution)/shard_map/all_to_all | solution.py:137
  31.1 89.6 %reduce-scatter.2.cloned.1.call-start = ((), (), s32[]{:S(2)}) async-start(), calls=%async_computation.3 | async-start | bytes 5111808 | tf_op jit(solution)/shard_map/reduce_scatter | solution.py:168
  41.3 3.2 %collective-permute-start = (bf16[288,128]{1,0:T(8,128)(2,1)S(1)}, bf16[288,128]{1,0:T(8,128)(2,1)S(1)}, u32[]{:S(2)}, u32[]{:S(2)}) collective-permute-start(bf16[288,128]{1,0:T(8,128)(2,1)S(1)} %bitcast.40), channel_id=1, source_target_pairs={{0,32},{32,0},{1,33},{33,1},{2,34},{34,2},{3,35},{35,3},{4,36},{36... | collective-permute-start | bytes 221192 | tf_op jit(solution)/shard_map/ppermute | solution.py:155
  55.6 8.5 %copy-start.1 = (f32[128,1]{1,0:T(8,128)S(1)}, f32[128,1]{1,0:T(8,128)}, u32[]{:S(2)}) copy-start(f32[128,1]{1,0:T(8,128)} %get-tuple-element.11) | copy-start | bytes 1540
  57.2 55.9 %all-to-all-start.1 = ((bf16[32,128,256]{2,1,0:T(8,128)(2,1)}), bf16[32,128,256]{2,1,0:T(8,128)(2,1)S(1)}, u32[]{:S(2)}, u32[]{:S(2)}) async-start(bf16[32,128,256]{2,1,0:T(8,128)(2,1)} %bitcast.36), calls=%async_computation.1 | async-start | bytes 4194304 | tf_op jit(solution)/shard_map/all_to_all | solution.py:162
Sparse Core Ops, SparseCore 0:
  50.4 70.2 reduce-scatter.1
